TPU v7x, 256 devices: a whole 4x4x8 slice. The times are simulated.
256 devices in a mesh: band: 16 (over z, x_hi), fft: 16 (over x_lo, y, core).
Axes of the slice: x: 4 (x_hi: 2, x_lo: 2; x = x_hi * 2 + x_lo), y: 4, z: 8, core: 2. Of those that a mesh axis runs over, the one named last changes fastest.
Arguments:
- orbitals: bfloat16 [32, 128, 128, 128], P('band', 'fft'), may hold values from -6 to 6
- owner_order: int32 [2], replicated, may hold values from 0 to 15, as said below
- sphere_mask: int32 [128, 128, 128], P(None, 'fft'), may hold values from 0 to 1, as said below
Outputs:
- fock_images: float32 [32, 128, 128, 128], P('band', 'fft')
Inputs may be any that keep to these rules, and one draw needn't show every extreme that they name: `owner_order`: the 2 owner groups are all different, and group 16 - 1 owns one of the rounds. `sphere_mask`: zero wherever q of the steps is less than the square of 56.
All inputs are finite; a program needn't handle non-finite values.
Results may differ from a plain program's by a relative error of at most 0.018.
Values may be sent and summed in bfloat16 or wider, within the bound.
A program may use at most 64 MiB of HBM per device.

v0:
```python
import math
import jax
import jax.numpy as jnp
from jax import lax
from jax.sharding import PartitionSpec as P

ROUNDS = 2


def spread(block, axis, source):
    block = jnp.where(lax.axis_index(axis) == source, block, jnp.zeros_like(block))
    return lax.psum(block, axis)


def dft_tables(points):
    rows_index = lax.broadcasted_iota(jnp.int32, (points, points), 0)
    cols_index = lax.broadcasted_iota(jnp.int32, (points, points), 1)
    phases = 2.0 * math.pi / points * (rows_index * cols_index % points).astype(jnp.float32)
    cosine = jnp.cos(phases)
    sine = jnp.sin(phases)
    forward_x = jnp.concatenate(
        [jnp.concatenate([cosine, -sine], 1), jnp.concatenate([sine, cosine], 1)], 0
    )
    inverse_x = jnp.concatenate(
        [jnp.concatenate([cosine, sine], 1), jnp.concatenate([-sine, cosine], 1)], 0
    )
    stacked = jnp.concatenate([cosine, sine], 0)
    return (
        forward_x.astype(jnp.bfloat16),
        inverse_x.astype(jnp.bfloat16),
        stacked.astype(jnp.bfloat16),
    )


def coulomb_slab(sphere_mask):
    points = sphere_mask.shape[0]
    width = sphere_mask.shape[1]
    shape = sphere_mask.shape
    along_z = lax.broadcasted_iota(jnp.int32, shape, 0)
    along_y = lax.broadcasted_iota(jnp.int32, shape, 1) + lax.axis_index("fft") * width
    along_x = lax.broadcasted_iota(jnp.int32, shape, 2)

    def signed(values):
        return jnp.where(values < points // 2, values, values - points)

    freq_z, freq_y, freq_x = (signed(along_z), signed(along_y), signed(along_x))
    total_sq = freq_z * freq_z + freq_y * freq_y + freq_x * freq_x
    inverse = jnp.where(
        total_sq > 0, 1.0 / jnp.maximum(total_sq, 1).astype(jnp.float32), jnp.float32(0.0)
    )
    return sphere_mask.astype(jnp.float32) * inverse * jnp.float32(1.0 / (3.0 * float(points)))


def combine_parts(cos_part, sin_part, direction):
    halfway = cos_part.shape[-1] // 2
    real_part = cos_part[..., :halfway] + direction * sin_part[..., halfway:]
    imag_part = cos_part[..., halfway:] - direction * sin_part[..., :halfway]
    return jnp.concatenate([real_part, imag_part], axis=-1)


def along_rows(values_in, stacked, direction):
    points = stacked.shape[1]
    result = jnp.einsum("ay,fzyc->fzac", stacked, values_in, preferred_element_type=jnp.float32)
    return combine_parts(result[:, :, :points], result[:, :, points:], direction)


def along_columns(values_in, stacked, direction):
    points = stacked.shape[1]
    result = jnp.einsum("az,fzmc->famc", stacked, values_in, preferred_element_type=jnp.float32)
    return combine_parts(result[:, :points], result[:, points:], direction)


def respond_many(first_ones, second_ones, locals_in, tables, kernel, outward, return_trip):
    forward_x, inverse_x, stacked = tables
    points = kernel.shape[-1]
    count = locals_in.shape[0]
    packs = first_ones.shape[0]
    local_values = locals_in.astype(jnp.float32)[:, None]
    firsts = first_ones.astype(jnp.float32)[None]
    seconds = second_ones.astype(jnp.float32)[None]
    packed = jnp.concatenate(
        [
            (firsts * local_values).astype(jnp.bfloat16),
            (seconds * local_values).astype(jnp.bfloat16),
        ],
        axis=-1,
    )
    packed = packed.reshape((count * packs,) + packed.shape[2:])
    section_one = jnp.dot(packed, forward_x, preferred_element_type=jnp.float32).astype(
        jnp.bfloat16
    )
    section_two = along_rows(section_one, stacked, 1.0).astype(jnp.bfloat16)
    columns_data = outward(section_two)
    spectrum = along_columns(columns_data, stacked, 1.0)
    split_shape = spectrum.shape[:3] + (2, points)
    section_three = (
        (spectrum.reshape(split_shape) * kernel[:, :, None, :])
        .reshape(spectrum.shape)
        .astype(jnp.bfloat16)
    )
    section_four = along_columns(section_three, stacked, -1.0).astype(jnp.bfloat16)
    planes_data = return_trip(section_four)
    section_five = along_rows(planes_data, stacked, -1.0).astype(jnp.bfloat16)
    section_six = jnp.dot(section_five, inverse_x, preferred_element_type=jnp.float32)
    section_six = section_six.reshape((count, packs) + section_six.shape[1:])
    return -jnp.sum(
        firsts * section_six[..., :points] + seconds * section_six[..., points:], axis=1
    )


def shards(orbitals, owner_order, sphere_mask):
    points = orbitals.shape[-1]
    tables = dft_tables(points)
    kernel = coulomb_slab(sphere_mask)
    owner_list = []
    for round_index in range(ROUNDS):
        owner_list.append(spread(orbitals, "band", owner_order[round_index]))

    def outward(values_in):
        return lax.all_to_all(values_in, "fft", split_axis=2, concat_axis=1, tiled=True)

    def return_trip(values_in):
        return lax.all_to_all(values_in, "fft", split_axis=1, concat_axis=2, tiled=True)

    accumulated = jnp.zeros(orbitals.shape, jnp.float32)
    for round_index in range(ROUNDS):
        owner_rows = owner_list[round_index]
        first_ones = owner_rows[0::2]
        second_ones = owner_rows[1::2]

        def band_step(carry, local):
            return (
                carry,
                respond_many(
                    first_ones, second_ones, local[None], tables, kernel, outward, return_trip
                )[0],
            )

        unused, contributions = lax.scan(band_step, None, orbitals)
        accumulated = accumulated + contributions
    return accumulated


def solution(mesh):
    placed = (P("band", "fft", None, None), P(), P(None, "fft", None))
    return jax.shard_map(
        shards, mesh=mesh, in_specs=placed, out_specs=P("band", "fft", None, None), check_vma=False
    )
```

profile of v0, /device:TPU:1, one launch (start us, length us, event | category | flops | bytes accessed | tf_op | source)
XLA Modules:
  0.0 341.3 jit_solution(6651478727574558865)
XLA Ops:
  9.1 2.1 broadcast_select_fusion
  13.2 152.5 %all-reduce.3.cloned.1.call-done = (bf16[2,8,128,128]{3,2,1,0:T(8,128)(2,1)}, bf16[2,8,128,128]{3,2,1,0:T(8,128)(2,1)}) async-done(((bf16[2,8,128,128]{3,2,1,0:T(8,128)(2,1)}, bf16[2,8,128,128]{3,2,1,0:T(8,128)(2,1)}), (bf16[2,8,128,128]{3,2,1,0:T(8,128)(2,1)}, bf16[2,8,128,128]{3,2,1,0:T(8,128)(2,1)})) %all-reduce.3.cloned.1.call-update) | async-done | bytes 1048592 | tf_op jit(solution)/shard_map/psum | solution.py:12
  168.0 87.5 %while.21 = (s32[]{:T(128)}, f32[2,8,128,128]{3,2,1,0:T(8,128)}, bf16[1,8,128,128]{3,2,1,0:T(8,128)(2,1)S(1)}, bf16[2,8,128,128]{3,2,1,0:T(8,128)(2,1)}, bf16[1,...) while((s32[]{:T(128)}, f32[2,8,128,128]{3,2,1,0:T(8,128)}, ...), condition=%wide.region_5.6_spmd, body=%wide.region_4.5_spmd.sunk | while | flops 814612480 | bytes 49021216 | solution.py:139
  168.0 2.0 fusion.159
  170.0 1.9 convolution_bitcast_fusion.25
  172.5 25.0 %all_to_all.57 = bf16[1,8,128,256]{3,1,0,2:T(8,128)(2,1)S(1)} all-to-all(bf16[1,8,128,256]{3,1,0,2:T(8,128)(2,1)S(1)} %copy.87), channel_id=1, replica_groups=mesh['band'=16,'fft'=16] {'fft'}, dimensions={2} | all-to-all | bytes 1048576 | tf_op jit(solution)/shard_map/while/body/eval_jaxpr/all_to_all | solution.py:120
  200.3 4.5 %all-to-all-start.3 = ((bf16[1,128,8,256]{3,2,0,1:T(8,128)(2,1)}), bf16[1,128,8,256]{3,2,0,1:T(8,128)(2,1)S(1)}, u32[]{:S(2)}, u32[]{:S(2)}) async-start(bf16[1,128,8,256]{3,2,0,1:T(8,128)(2,1)} %copy.90), calls=%async_computation.3 | async-start | bytes 1048576 | tf_op jit(solution)/shard_map/while/body/eval_jaxpr/all_to_all | solution.py:123
  204.8 9.9 %all-to-all-done.3 = bf16[1,128,8,256]{3,2,0,1:T(8,128)(2,1)S(1)} async-done(((bf16[1,128,8,256]{3,2,0,1:T(8,128)(2,1)}), bf16[1,128,8,256]{3,2,0,1:T(8,128)(2,1)S(1)}, u32[]{:S(2)}, u32[]{:S(2)}) %all-to-all-start.3) | async-done | bytes 524320 | tf_op jit(solution)/shard_map/while/body/eval_jaxpr/all_to_all | solution.py:123
  217.5 2.0 fusion.159
  219.5 1.9 convolution_bitcast_fusion.25
  222.0 13.5 %all_to_all.57 = bf16[1,8,128,256]{3,1,0,2:T(8,128)(2,1)S(1)} all-to-all(bf16[1,8,128,256]{3,1,0,2:T(8,128)(2,1)S(1)} %copy.87), channel_id=1, replica_groups=mesh['band'=16,'fft'=16] {'fft'}, dimensions={2} | all-to-all | bytes 1048576 | tf_op jit(solution)/shard_map/while/body/eval_jaxpr/all_to_all | solution.py:120
  238.2 4.5 %all-to-all-start.3 = ((bf16[1,128,8,256]{3,2,0,1:T(8,128)(2,1)}), bf16[1,128,8,256]{3,2,0,1:T(8,128)(2,1)S(1)}, u32[]{:S(2)}, u32[]{:S(2)}) async-start(bf16[1,128,8,256]{3,2,0,1:T(8,128)(2,1)} %copy.90), calls=%async_computation.3 | async-start | bytes 1048576 | tf_op jit(solution)/shard_map/while/body/eval_jaxpr/all_to_all | solution.py:123
  242.7 9.9 %all-to-all-done.3 = bf16[1,128,8,256]{3,2,0,1:T(8,128)(2,1)S(1)} async-done(((bf16[1,128,8,256]{3,2,0,1:T(8,128)(2,1)}), bf16[1,128,8,256]{3,2,0,1:T(8,128)(2,1)S(1)}, u32[]{:S(2)}, u32[]{:S(2)}) %all-to-all-start.3) | async-done | bytes 524320 | tf_op jit(solution)/shard_map/while/body/eval_jaxpr/all_to_all | solution.py:123
  256.6 75.2 %while.20 = (s32[]{:T(128)}, f32[2,8,128,128]{3,2,1,0:T(8,128)}, bf16[1,8,128,128]{3,2,1,0:T(8,128)(2,1)S(1)}, bf16[2,8,128,128]{3,2,1,0:T(8,128)(2,1)}, bf16[1,...) while((s32[]{:T(128)}, f32[2,8,128,128]{3,2,1,0:T(8,128)}, ...), condition=%wide.region_2.3_spmd, body=%wide.region_1.2_spmd.sunk | while | flops 814612480 | bytes 46924008 | solution.py:139
  256.6 1.8 fusion.142
  258.4 1.8 convolution_bitcast_fusion.20
  260.7 13.5 %all_to_all.56 = bf16[1,8,128,256]{3,1,0,2:T(8,128)(2,1)S(1)} all-to-all(bf16[1,8,128,256]{3,1,0,2:T(8,128)(2,1)S(1)} %copy.81), channel_id=1, replica_groups=mesh['band'=16,'fft'=16] {'fft'}, dimensions={2} | all-to-all | bytes 1048576 | tf_op jit(solution)/shard_map/while/body/eval_jaxpr/all_to_all | solution.py:120
  277.0 4.5 %all-to-all-start.1 = ((bf16[1,128,8,256]{3,2,0,1:T(8,128)(2,1)}), bf16[1,128,8,256]{3,2,0,1:T(8,128)(2,1)S(1)}, u32[]{:S(2)}, u32[]{:S(2)}) async-start(bf16[1,128,8,256]{3,2,0,1:T(8,128)(2,1)} %copy.84), calls=%async_computation.1 | async-start | bytes 1048576 | tf_op jit(solution)/shard_map/while/body/eval_jaxpr/all_to_all | solution.py:123
  281.5 9.9 %all-to-all-done.1 = bf16[1,128,8,256]{3,2,0,1:T(8,128)(2,1)S(1)} async-done(((bf16[1,128,8,256]{3,2,0,1:T(8,128)(2,1)}), bf16[1,128,8,256]{3,2,0,1:T(8,128)(2,1)S(1)}, u32[]{:S(2)}, u32[]{:S(2)}) %all-to-all-start.1) | async-done | bytes 524320 | tf_op jit(solution)/shard_map/while/body/eval_jaxpr/all_to_all | solution.py:123
  296.0 1.8 convolution_bitcast_fusion.20
  298.3 13.5 %all_to_all.56 = bf16[1,8,128,256]{3,1,0,2:T(8,128)(2,1)S(1)} all-to-all(bf16[1,8,128,256]{3,1,0,2:T(8,128)(2,1)S(1)} %copy.81), channel_id=1, replica_groups=mesh['band'=16,'fft'=16] {'fft'}, dimensions={2} | all-to-all | bytes 1048576 | tf_op jit(solution)/shard_map/while/body/eval_jaxpr/all_to_all | solution.py:120
  314.6 4.5 %all-to-all-start.1 = ((bf16[1,128,8,256]{3,2,0,1:T(8,128)(2,1)}), bf16[1,128,8,256]{3,2,0,1:T(8,128)(2,1)S(1)}, u32[]{:S(2)}, u32[]{:S(2)}) async-start(bf16[1,128,8,256]{3,2,0,1:T(8,128)(2,1)} %copy.84), calls=%async_computation.1 | async-start | bytes 1048576 | tf_op jit(solution)/shard_map/while/body/eval_jaxpr/all_to_all | solution.py:123
  319.1 9.9 %all-to-all-done.1 = bf16[1,128,8,256]{3,2,0,1:T(8,128)(2,1)S(1)} async-done(((bf16[1,128,8,256]{3,2,0,1:T(8,128)(2,1)}), bf16[1,128,8,256]{3,2,0,1:T(8,128)(2,1)S(1)}, u32[]{:S(2)}, u32[]{:S(2)}) %all-to-all-start.1) | async-done | bytes 524320 | tf_op jit(solution)/shard_map/while/body/eval_jaxpr/all_to_all | solution.py:123
  331.8 2.6 add.91
  (115 shorter events, 32.6 us)
Async XLA Ops:
  6.5 4.7 %copy-start.8 = (s32[128,8,128]{2,1,0:T(8,128)S(1)}, s32[128,8,128]{2,1,0:T(8,128)}, u32[]{:S(2)}) copy-start(s32[128,8,128]{2,1,0:T(8,128)} %param.9) | copy-start | bytes 1572868
  6.5 159.1 %all-reduce.3.cloned.1.call-start = ((), (), s32[]{:S(2)}) async-start(), calls=%async_computation.4 | async-start | bytes 2097152 | tf_op jit(solution)/shard_map/psum | solution.py:12
  168.0 2.0 copy-start
  200.3 14.4 %all-to-all-start.3 = ((bf16[1,128,8,256]{3,2,0,1:T(8,128)(2,1)}), bf16[1,128,8,256]{3,2,0,1:T(8,128)(2,1)S(1)}, u32[]{:S(2)}, u32[]{:S(2)}) async-start(bf16[1,128,8,256]{3,2,0,1:T(8,128)(2,1)} %copy.90), calls=%async_computation.3 | async-start | bytes 1048576 | tf_op jit(solution)/shard_map/while/body/eval_jaxpr/all_to_all | solution.py:123
  214.7 0.9 copy-start.2
  215.1 1.0 copy-start.1
  215.1 1.3 copy-start.6
  216.6 1.0 copy-start.7
  217.5 2.0 copy-start
  238.2 14.4 %all-to-all-start.3 = ((bf16[1,128,8,256]{3,2,0,1:T(8,128)(2,1)}), bf16[1,128,8,256]{3,2,0,1:T(8,128)(2,1)S(1)}, u32[]{:S(2)}, u32[]{:S(2)}) async-start(bf16[1,128,8,256]{3,2,0,1:T(8,128)(2,1)} %copy.90), calls=%async_computation.3 | async-start | bytes 1048576 | tf_op jit(solution)/shard_map/while/body/eval_jaxpr/all_to_all | solution.py:123
  252.6 0.9 copy-start.2
  253.1 1.0 copy-start.1
  253.1 1.3 copy-start.6
  254.5 1.0 copy-start.7
  277.0 14.4 %all-to-all-start.1 = ((bf16[1,128,8,256]{3,2,0,1:T(8,128)(2,1)}), bf16[1,128,8,256]{3,2,0,1:T(8,128)(2,1)S(1)}, u32[]{:S(2)}, u32[]{:S(2)}) async-start(bf16[1,128,8,256]{3,2,0,1:T(8,128)(2,1)} %copy.84), calls=%async_computation.1 | async-start | bytes 1048576 | tf_op jit(solution)/shard_map/while/body/eval_jaxpr/all_to_all | solution.py:123
  291.4 0.9 copy-start.3
  291.9 1.2 copy-start.4
  293.2 1.0 copy-start.5
  314.6 14.4 %all-to-all-start.1 = ((bf16[1,128,8,256]{3,2,0,1:T(8,128)(2,1)}), bf16[1,128,8,256]{3,2,0,1:T(8,128)(2,1)S(1)}, u32[]{:S(2)}, u32[]{:S(2)}) async-start(bf16[1,128,8,256]{3,2,0,1:T(8,128)(2,1)} %copy.84), calls=%async_computation.1 | async-start | bytes 1048576 | tf_op jit(solution)/shard_map/while/body/eval_jaxpr/all_to_all | solution.py:123
  329.0 0.9 copy-start.3
  329.5 1.2 copy-start.4
  330.8 1.0 copy-start.5
Sparse Core Ops, SparseCore 0:
  11.4 154.2 all-reduce.2
where the time goes:
time: 342 us; the launch traced here: 341 us
  waiting for transfers between devices  192 us (56%)
  blocking collectives  65.5 us (19%)
  local copies, waits for them, and re-layouts  18.9 us (6%)
  starting transfers between devices  18.1 us (5%)
  other arithmetic  17.3 us (5%)
  between operations  14.8 us (4%)
  matrix products  14.2 us (4%)
    psum x1, waiting for transfers between devices, spread(): return lax.psum(block, axis)  153 us
    all_to_all x4, blocking collectives, outward(): lax.all_to_all(values_in, 'fft', split_axis=2, concat_axis=1, tiled=True)  65.5 us
    all_to_all x4, waiting for transfers between devices, return_trip(): lax.all_to_all(values_in, 'fft', split_axis=1, concat_axis=2, tiled=True)  39.5 us
    all_to_all x4, starting transfers between devices, return_trip(): lax.all_to_all(values_in, 'fft', split_axis=1, concat_axis=2, tiled=True)  18.1 us
    dot_general x8, matrix products, along_rows(): jnp.einsum('ay,fzyc->fzac', stacked, values_in, preferred_element_type=jn...  9.2 us
    convert_element_type x4, other arithmetic, respond_many(): (firsts * local_values).astype(jnp.bfloat16)  7.5 us
    while x32, local copies, waits for them, and re-layouts  6.97 us
  transfers between devices with their start and end apart: 5, of which 5 were waited for; matrix products, arithmetic and copies ran while one was open for 1% of the time, Pallas kernels for 0%

commit v1 on v0

--- a/solution.py
+++ b/solution.py
@@ -9,7 +9,7 @@
 
 def spread(block, axis, source):
     block = jnp.where(lax.axis_index(axis) == source, block, jnp.zeros_like(block))
-    return lax.psum(block, axis)
+    return jnp.sum(lax.all_gather(block, axis), axis=0)
 
 
 def dft_tables(points):

time: 342 us -> 457 us (1.34)
  waiting for transfers between devices: 192 us -> 307 us
  other arithmetic: 17.3 us -> 27.8 us
  blocking collectives: 65.5 us -> 55.4 us
    all_gather x0 -> x2, waiting for transfers between devices: none -> 267 us  [spread(): return jnp.sum(lax.all_gather(block, axis), axis=0)]
    psum x1 -> x0, waiting for transfers between devices: 153 us -> none  [spread(): return lax.psum(block, axis)]
    reduce_sum x0 -> x2, other arithmetic: none -> 10.5 us  [spread(): return jnp.sum(lax.all_gather(block, axis), axis=0)]
    all_to_all x4, blocking collectives: 65.5 us -> 55.4 us  [outward(): lax.all_to_all(values_in, 'fft', split_axis=2, concat_axis=1, tiled=True)]
  transfers between devices with their start and end apart: 5 -> 6, of which waited for: 5 -> 6; matrix products, arithmetic and copies ran while one was open for 1% -> 2% of each run, Pallas kernels for 0% -> 0%
where the time goes in v1:
time: 457 us; the launch traced here: 455 us
  waiting for transfers between devices  307 us (67%)
  blocking collectives  55.4 us (12%)
  other arithmetic  27.8 us (6%)
  starting transfers between devices  18.1 us (4%)
  local copies, waits for them, and re-layouts  17.8 us (4%)
  between operations  14.7 us (3%)
  matrix products  14.2 us (3%)
    all_gather x2, waiting for transfers between devices, spread(): return jnp.sum(lax.all_gather(block, axis), axis=0)  267 us
    all_to_all x4, blocking collectives, outward(): lax.all_to_all(values_in, 'fft', split_axis=2, concat_axis=1, tiled=True)  55.4 us
    all_to_all x4, waiting for transfers between devices, return_trip(): lax.all_to_all(values_in, 'fft', split_axis=1, concat_axis=2, tiled=True)  39.5 us
    all_to_all x4, starting transfers between devices, return_trip(): lax.all_to_all(values_in, 'fft', split_axis=1, concat_axis=2, tiled=True)  18.1 us
    reduce_sum x2, other arithmetic, spread(): return jnp.sum(lax.all_gather(block, axis), axis=0)  10.5 us
    dot_general x8, matrix products, along_rows(): jnp.einsum('ay,fzyc->fzac', stacked, values_in, preferred_element_type=jn...  9.21 us
  transfers between devices with their start and end apart: 6, of which 6 were waited for; matrix products, arithmetic and copies ran while one was open for 2% of the time, Pallas kernels for 0%

profile of v1, /device:TPU:1, one launch (start us, length us, event | category | flops | bytes accessed | tf_op | source)
XLA Modules:
  0.0 455.5 jit_solution(11976078944982327982)
XLA Ops:
  9.1 2.1 broadcast_select_fusion
  13.8 136.7 %all-gather.7.cloned.1.call-done = bf16[32,8,128,128]{3,2,1,0:T(8,128)(2,1)} async-done(((bf16[2,8,128,128]{3,2,1,0:T(8,128)(2,1)}), bf16[32,8,128,128]{3,2,1,0:T(8,128)(2,1)}) %all-gather.7.cloned.1.call-update) | async-done | bytes 8388624 | tf_op jit(solution)/shard_map/all_gather | solution.py:12
  150.6 5.3 %reduce_sum.33 = bf16[2,8,128,128]{3,2,1,0:T(8,128)(2,1)S(1)} reduce(bf16[16,2,8,128,128]{4,3,2,1,0:T(8,128)(2,1)} %bitcast.264, bf16[]{:T(256)} %constant.62.clone.1), dimensions={0}, to_apply=%region_3.4 | reduce | flops 3932160 | bytes 8912898 | tf_op jit(solution)/shard_map/reduce_sum | solution.py:12
  155.9 130.0 %all-gather.5.cloned.1.call-done = bf16[32,8,128,128]{3,2,1,0:T(8,128)(2,1)} async-done(((bf16[2,8,128,128]{3,2,1,0:T(8,128)(2,1)}), bf16[32,8,128,128]{3,2,1,0:T(8,128)(2,1)}) %all-gather.5.cloned.1.call-update) | async-done | bytes 8388624 | tf_op jit(solution)/shard_map/all_gather | solution.py:12
  285.8 5.3 %reduce_sum.32 = bf16[2,8,128,128]{3,2,1,0:T(8,128)(2,1)S(1)} reduce(bf16[16,2,8,128,128]{4,3,2,1,0:T(8,128)(2,1)} %bitcast.265, bf16[]{:T(256)} %constant.62.clone.1), dimensions={0}, to_apply=%region_0.1 | reduce | flops 3932160 | bytes 8912898 | tf_op jit(solution)/shard_map/reduce_sum | solution.py:12
  292.2 77.5 %while.20 = (s32[]{:T(128)}, f32[2,8,128,128]{3,2,1,0:T(8,128)}, bf16[1,8,128,128]{3,2,1,0:T(8,128)(2,1)S(1)}, bf16[2,8,128,128]{3,2,1,0:T(8,128)(2,1)}, bf16[1,...) while((s32[]{:T(128)}, f32[2,8,128,128]{3,2,1,0:T(8,128)}, ...), condition=%wide.region_2.3_spmd, body=%wide.region_1.2_spmd.sunk | while | flops 814612480 | bytes 49021216 | solution.py:139
  292.2 2.0 fusion.142
  294.2 1.9 convolution_bitcast_fusion.20
  296.7 15.0 %all_to_all.56 = bf16[1,8,128,256]{3,1,0,2:T(8,128)(2,1)S(1)} all-to-all(bf16[1,8,128,256]{3,1,0,2:T(8,128)(2,1)S(1)} %copy.81), channel_id=1, replica_groups=mesh['band'=16,'fft'=16] {'fft'}, dimensions={2} | all-to-all | bytes 1048576 | tf_op jit(solution)/shard_map/while/body/eval_jaxpr/all_to_all | solution.py:120
  314.4 4.5 all-to-all-start.1
  318.9 9.9 %all-to-all-done.1 = bf16[1,128,8,256]{3,2,0,1:T(8,128)(2,1)S(1)} async-done(((bf16[1,128,8,256]{3,2,0,1:T(8,128)(2,1)}), bf16[1,128,8,256]{3,2,0,1:T(8,128)(2,1)S(1)}, u32[]{:S(2)}, u32[]{:S(2)}) %all-to-all-start.1) | async-done | bytes 524320 | tf_op jit(solution)/shard_map/while/body/eval_jaxpr/all_to_all | solution.py:123
  331.7 2.0 fusion.142
  333.7 1.9 convolution_bitcast_fusion.20
  336.1 13.5 %all_to_all.56 = bf16[1,8,128,256]{3,1,0,2:T(8,128)(2,1)S(1)} all-to-all(bf16[1,8,128,256]{3,1,0,2:T(8,128)(2,1)S(1)} %copy.81), channel_id=1, replica_groups=mesh['band'=16,'fft'=16] {'fft'}, dimensions={2} | all-to-all | bytes 1048576 | tf_op jit(solution)/shard_map/while/body/eval_jaxpr/all_to_all | solution.py:120
  352.4 4.5 all-to-all-start.1
  356.9 9.9 %all-to-all-done.1 = bf16[1,128,8,256]{3,2,0,1:T(8,128)(2,1)S(1)} async-done(((bf16[1,128,8,256]{3,2,0,1:T(8,128)(2,1)}), bf16[1,128,8,256]{3,2,0,1:T(8,128)(2,1)S(1)}, u32[]{:S(2)}, u32[]{:S(2)}) %all-to-all-start.1) | async-done | bytes 524320 | tf_op jit(solution)/shard_map/while/body/eval_jaxpr/all_to_all | solution.py:123
  370.8 75.2 %while.21 = (s32[]{:T(128)}, f32[2,8,128,128]{3,2,1,0:T(8,128)}, bf16[1,8,128,128]{3,2,1,0:T(8,128)(2,1)S(1)}, bf16[2,8,128,128]{3,2,1,0:T(8,128)(2,1)}, bf16[1,...) while((s32[]{:T(128)}, f32[2,8,128,128]{3,2,1,0:T(8,128)}, ...), condition=%wide.region_5.6_spmd, body=%wide.region_4.5_spmd.sunk | while | flops 814612480 | bytes 46924008 | solution.py:139
  374.9 13.5 %all_to_all.57 = bf16[1,8,128,256]{3,1,0,2:T(8,128)(2,1)S(1)} all-to-all(bf16[1,8,128,256]{3,1,0,2:T(8,128)(2,1)S(1)} %copy.87), channel_id=1, replica_groups=mesh['band'=16,'fft'=16] {'fft'}, dimensions={2} | all-to-all | bytes 1048576 | tf_op jit(solution)/shard_map/while/body/eval_jaxpr/all_to_all | solution.py:120
  391.2 4.5 all-to-all-start.3
  395.7 9.9 %all-to-all-done.3 = bf16[1,128,8,256]{3,2,0,1:T(8,128)(2,1)S(1)} async-done(((bf16[1,128,8,256]{3,2,0,1:T(8,128)(2,1)}), bf16[1,128,8,256]{3,2,0,1:T(8,128)(2,1)S(1)}, u32[]{:S(2)}, u32[]{:S(2)}) %all-to-all-start.3) | async-done | bytes 524320 | tf_op jit(solution)/shard_map/while/body/eval_jaxpr/all_to_all | solution.py:123
  412.6 13.5 %all_to_all.57 = bf16[1,8,128,256]{3,1,0,2:T(8,128)(2,1)S(1)} all-to-all(bf16[1,8,128,256]{3,1,0,2:T(8,128)(2,1)S(1)} %copy.87), channel_id=1, replica_groups=mesh['band'=16,'fft'=16] {'fft'}, dimensions={2} | all-to-all | bytes 1048576 | tf_op jit(solution)/shard_map/while/body/eval_jaxpr/all_to_all | solution.py:120
  428.8 4.5 all-to-all-start.3
  433.3 9.9 %all-to-all-done.3 = bf16[1,128,8,256]{3,2,0,1:T(8,128)(2,1)S(1)} async-done(((bf16[1,128,8,256]{3,2,0,1:T(8,128)(2,1)}), bf16[1,128,8,256]{3,2,0,1:T(8,128)(2,1)S(1)}, u32[]{:S(2)}, u32[]{:S(2)}) %all-to-all-start.3) | async-done | bytes 524320 | tf_op jit(solution)/shard_map/while/body/eval_jaxpr/all_to_all | solution.py:123
  446.0 2.6 add.87
  (121 shorter events, 37.6 us)
Async XLA Ops:
  6.5 5.4 %copy-start.8 = (s32[128,8,128]{2,1,0:T(8,128)S(1)}, s32[128,8,128]{2,1,0:T(8,128)}, u32[]{:S(2)}) copy-start(s32[128,8,128]{2,1,0:T(8,128)} %param.9) | copy-start | bytes 1572868
  6.5 144.0 %all-gather.7.cloned.1.call-start = ((), (), s32[]{:S(2)}) async-start(), calls=%async_computation.5 | async-start | bytes 8912896 | tf_op jit(solution)/shard_map/all_gather | solution.py:12
  11.2 274.6 %all-gather.5.cloned.1.call-start = ((), (), s32[]{:S(2)}) async-start(), calls=%async_computation.4 | async-start | bytes 8912896 | tf_op jit(solution)/shard_map/all_gather | solution.py:12
  292.2 2.0 copy-start
  314.4 14.4 %all-to-all-start.1 = ((bf16[1,128,8,256]{3,2,0,1:T(8,128)(2,1)}), bf16[1,128,8,256]{3,2,0,1:T(8,128)(2,1)S(1)}, u32[]{:S(2)}, u32[]{:S(2)}) async-start(bf16[1,128,8,256]{3,2,0,1:T(8,128)(2,1)} %copy.84), calls=%async_computation.1 | async-start | bytes 1048576 | tf_op jit(solution)/shard_map/while/body/eval_jaxpr/all_to_all | solution.py:123
  328.8 0.9 copy-start.2
  329.3 1.0 copy-start.1
  329.3 1.3 copy-start.6
  330.7 1.0 copy-start.7
  331.7 2.0 copy-start
  352.4 14.4 %all-to-all-start.1 = ((bf16[1,128,8,256]{3,2,0,1:T(8,128)(2,1)}), bf16[1,128,8,256]{3,2,0,1:T(8,128)(2,1)S(1)}, u32[]{:S(2)}, u32[]{:S(2)}) async-start(bf16[1,128,8,256]{3,2,0,1:T(8,128)(2,1)} %copy.84), calls=%async_computation.1 | async-start | bytes 1048576 | tf_op jit(solution)/shard_map/while/body/eval_jaxpr/all_to_all | solution.py:123
  366.8 0.9 copy-start.2
  367.3 1.0 copy-start.1
  367.3 1.3 copy-start.6
  368.7 1.0 copy-start.7
  391.2 14.4 %all-to-all-start.3 = ((bf16[1,128,8,256]{3,2,0,1:T(8,128)(2,1)}), bf16[1,128,8,256]{3,2,0,1:T(8,128)(2,1)S(1)}, u32[]{:S(2)}, u32[]{:S(2)}) async-start(bf16[1,128,8,256]{3,2,0,1:T(8,128)(2,1)} %copy.90), calls=%async_computation.3 | async-start | bytes 1048576 | tf_op jit(solution)/shard_map/while/body/eval_jaxpr/all_to_all | solution.py:123
  405.6 0.9 copy-start.3
  406.1 1.2 copy-start.4
  407.4 1.0 copy-start.5
  428.8 14.4 %all-to-all-start.3 = ((bf16[1,128,8,256]{3,2,0,1:T(8,128)(2,1)}), bf16[1,128,8,256]{3,2,0,1:T(8,128)(2,1)S(1)}, u32[]{:S(2)}, u32[]{:S(2)}) async-start(bf16[1,128,8,256]{3,2,0,1:T(8,128)(2,1)} %copy.90), calls=%async_computation.3 | async-start | bytes 1048576 | tf_op jit(solution)/shard_map/while/body/eval_jaxpr/all_to_all | solution.py:123
  443.2 0.9 copy-start.3
  443.7 1.2 copy-start.4
  445.0 1.0 copy-start.5
Sparse Core Ops, SparseCore 0:
  11.3 139.1 all-gather.6
  153.1 132.6 all-gather.4
